TPU v7x, 256 devices: a whole 4x4x8 slice. The times are simulated.
256 devices in a mesh: blk: 8 (over x, core), uly: 8 (over z), tp: 4 (over y).
Axes of the slice: x: 4, y: 4, z: 8, core: 2. Of those that a mesh axis runs over, the one named last changes fastest.
Arguments:
- hidden: bfloat16 [8192, 8192], P(('blk', 'uly')), may hold values from -8 to 8
- norm_gain: bfloat16 [8192], replicated, may hold values from 0.099609375 to 1.8984375
- query_key_value_weight: bfloat16 [8192, 4, 1280], P('uly', 'tp'), may hold values from -1 to 1
- w_out: bfloat16 [4096, 8192], P('tp', 'uly'), may hold values from -0.5 to 0.5
- doc_ids: int32 [8192], replicated, may hold values from 0 to 15, never falling along the last dimension, each value on 1 to 2048 neighbouring positions
- block_order: int32 [16], replicated, may hold values from 0 to 15, each once
Outputs:
- attn_out: bfloat16 [8192, 8192], P(('blk', 'tp'), 'uly')
Inputs may be any that keep to these rules, and one draw needn't show every extreme that they name: `doc_ids`: never falls along the sequence; every document holds 1 to 2048 positions and one holds exactly 2048. Array rows c * 512 to (c + 1) * 512 - 1 hold sequence block block_order[c]; every block appears once.
All inputs are finite; a program needn't handle non-finite values.
Results may differ from a plain program's by a relative error of at most 0.029.
Values may be sent and summed in bfloat16 or wider, within the bound.
A program may use at most 64 MiB of HBM per device.

v0:
```python
import math
import jax
import jax.numpy as jnp
from jax import lax
from jax.sharding import PartitionSpec as P

QUERY_HEAD_COUNT = 32
KV_HEAD_COUNT = 4
HEAD_SIZE = 128
BLOCK = 512
THETA = 500000.0
NEG_BIG = -1e30


def rope_tables(positions):
    half_dim = HEAD_SIZE // 2
    lane_ids = jnp.arange(half_dim).astype(jnp.float32)
    base_freq = jnp.power(THETA, -2.0 * lane_ids / HEAD_SIZE)
    wavelen = 2.0 * math.pi / base_freq
    smooth = (8192.0 / wavelen - 1.0) / 3.0
    blended = (1.0 - smooth) * base_freq / 8.0 + smooth * base_freq
    scaled = jnp.where(
        wavelen > 8192.0, base_freq / 8.0, jnp.where(wavelen < 2048.0, base_freq, blended)
    )
    angles = positions.astype(jnp.float32)[:, None] * scaled[None, :]
    return (jnp.cos(angles), jnp.sin(angles))


def rotate(values, cos_table, sin_table):
    half_dim = values.shape[-1] // 2
    leading = values[..., :half_dim]
    trailing = values[..., half_dim:]
    cos_part = cos_table[:, None, :]
    sin_part = sin_table[:, None, :]
    return jnp.concatenate(
        [leading * cos_part - trailing * sin_part, trailing * cos_part + leading * sin_part],
        axis=-1,
    )


def positions_of(block_order, row_ids):
    block_ids = row_ids // BLOCK
    matches = block_ids[:, None] == jnp.arange(block_order.shape[0])[None, :]
    seq_block = jnp.sum(jnp.where(matches, block_order[None, :], 0), axis=1)
    return seq_block * BLOCK + row_ids % BLOCK


def make_attend(queries, query_pos, query_seg, doc_ids, block_order):
    head_dim = queries.shape[2]
    inv_root = 1.0 / math.sqrt(head_dim)

    def attend(running, pieces, offset):
        key_piece, value_piece = pieces
        key_count = key_piece.shape[0]
        block_size = key_count
        while block_size > 1024 and block_size % 2 == 0:
            block_size = block_size // 2
        block_total = key_count // block_size
        piece_pos = positions_of(block_order, jnp.arange(key_count))
        piece_seg = jnp.take(doc_ids, piece_pos)
        stacked = (
            key_piece.reshape(block_total, block_size, head_dim),
            value_piece.reshape(block_total, block_size, head_dim),
            piece_pos.reshape(block_total, block_size),
            piece_seg.reshape(block_total, block_size),
        )

        def one_block(softmax_state, block_data):
            key_blk, value_blk, pos_blk, seg_blk = block_data
            allowed = (pos_blk[None, :] <= query_pos[:, None]) & (
                seg_blk[None, :] == query_seg[:, None]
            )
            row_max, row_sum, weighted = softmax_state
            scores = (
                jnp.einsum("qhd,kd->hqk", queries, key_blk, preferred_element_type=jnp.float32)
                * inv_root
            )
            scores = jnp.where(allowed[None, :, :], scores, NEG_BIG)
            new_max = jnp.maximum(row_max, jnp.max(scores, axis=2))
            weights = jnp.where(allowed[None, :, :], jnp.exp(scores - new_max[:, :, None]), 0.0)
            factor = jnp.exp(row_max - new_max)
            new_sum = row_sum * factor + jnp.sum(weights, axis=2)
            product = jnp.einsum(
                "hqk,kd->hqd",
                weights.astype(jnp.bfloat16),
                value_blk,
                preferred_element_type=jnp.float32,
            )
            next_state = (new_max, new_sum, weighted * factor[:, :, None] + product)
            return (next_state, None)

        final_state, unused = lax.scan(one_block, running, stacked)
        return final_state

    return attend


def on_device(hidden, norm_gain, query_key_value_weight, w_out, doc_ids, block_order):
    group_width = QUERY_HEAD_COUNT // KV_HEAD_COUNT
    heads_here = group_width // lax.axis_size("uly")
    widened = hidden.astype(jnp.float32)
    inverse_rms = lax.rsqrt(jnp.mean(widened * widened, axis=1, keepdims=True) + 1e-05)
    rms_scaled = (widened * inverse_rms * norm_gain.astype(jnp.float32)[None, :]).astype(
        jnp.bfloat16
    )
    regrouped = lax.all_to_all(rms_scaled, "uly", split_axis=1, concat_axis=0, tiled=True)
    block_len = regrouped.shape[0]
    local_weights = query_key_value_weight.reshape(
        query_key_value_weight.shape[0], (group_width + 2) * HEAD_SIZE
    )
    partial_proj = jnp.dot(regrouped, local_weights, preferred_element_type=jnp.float32)
    query_part = partial_proj[:, : group_width * HEAD_SIZE]
    pair_part = partial_proj[:, group_width * HEAD_SIZE :]
    first_row = lax.axis_index("blk") * block_len
    query_pos = positions_of(block_order, first_row + jnp.arange(block_len))
    query_seg = jnp.take(doc_ids, query_pos)
    cos_query, sin_query = rope_tables(query_pos)
    query_sum, pair_sum = (
        lax.psum_scatter(query_part, "uly", scatter_dimension=1, tiled=True),
        lax.psum_scatter(pair_part, "uly", scatter_dimension=0, tiled=True),
    )
    key_len = pair_sum.shape[0]
    key_start = first_row + lax.axis_index("uly") * key_len
    key_pos = positions_of(block_order, key_start + jnp.arange(key_len))
    cos_key, sin_key = rope_tables(key_pos)
    queries = rotate(
        query_sum.reshape(block_len, heads_here, HEAD_SIZE), cos_query, sin_query
    ).astype(jnp.bfloat16)
    keys_local = rotate(pair_sum[:, None, :HEAD_SIZE], cos_key, sin_key)[:, 0, :].astype(
        jnp.bfloat16
    )
    values_local = pair_sum[:, HEAD_SIZE:].astype(jnp.bfloat16)
    attend = make_attend(queries, query_pos, query_seg, doc_ids, block_order)
    initial = (
        jnp.full((heads_here, block_len), NEG_BIG, jnp.float32),
        jnp.zeros((heads_here, block_len), jnp.float32),
        jnp.zeros((heads_here, block_len, HEAD_SIZE), jnp.float32),
    )
    final_state = attend(
        initial,
        (
            lax.all_gather(keys_local, ("blk", "uly"), axis=0, tiled=True),
            lax.all_gather(values_local, ("blk", "uly"), axis=0, tiled=True),
        ),
        jnp.int32(0),
    )
    row_max, row_sum, weighted = final_state
    attended = (weighted / row_sum[:, :, None]).astype(jnp.bfloat16)
    head_weights = w_out.reshape(group_width, HEAD_SIZE, w_out.shape[1])
    projected_rows = jnp.einsum(
        "hqd,hdn->qn",
        lax.all_gather(attended, "uly", axis=0, tiled=True),
        head_weights,
        preferred_element_type=jnp.float32,
    )
    return lax.psum_scatter(
        projected_rows.astype(jnp.bfloat16), "tp", scatter_dimension=0, tiled=True
    )


def solution(mesh):
    return jax.shard_map(
        on_device,
        mesh=mesh,
        in_specs=(P(("blk", "uly"), None), P(), P("uly", "tp", None), P("tp", "uly"), P(), P()),
        out_specs=P(("blk", "tp"), "uly"),
        check_vma=False,
    )
```

profile of v0, /device:TPU:1, one launch (start us, length us, event | category | flops | bytes accessed | tf_op | source)
XLA Modules:
  0.0 473.3 jit_solution(8503466636216364546)
XLA Ops:
  6.5 0.9 convert_element_type.57
  7.4 4.1 copy.14
  11.5 2.7 fusion.26
  14.2 4.6 fusion.28
  18.8 58.6 %all_to_all.19 = bf16[128,8,1024]{0,2,1:T(8,128)(2,1)} all-to-all(bf16[128,8,1024]{0,2,1:T(8,128)(2,1)S(1)} %bitcast.99), channel_id=1, replica_groups=mesh['blk'=8,'uly'=8,'tp'=4] {'uly'}, dimensions={1} | all-to-all | bytes 4194304 | tf_op jit(solution)/shard_map/all_to_all | solution.py:106
  77.4 3.9 copy.15
  81.3 4.7 fusion.29
  86.0 2.3 copy-done.2
  88.2 1.1 slice.37
  89.3 0.0 reduce-scatter.4.cloned.1.call-update
  89.3 0.0 all-gather.9.cloned.1.call-start
  89.4 0.1 select_reduce_fusion.2
  89.6 32.3 %reduce-scatter.4.cloned.1.call-done = f32[128,256]{0,1:T(8,128)} async-done(((f32[1024,256]{0,1:T(8,128)}), f32[128,256]{0,1:T(8,128)}) %reduce-scatter.4.cloned.1.call-update) | async-done | bytes 131088 | tf_op jit(solution)/shard_map/reduce_scatter | solution.py:120
  121.8 0.8 slice_bitcast_fusion
  122.7 0.2 fusion.45
  122.9 0.6 pad_maximum_fusion.1
  123.5 0.0 all-gather.5.cloned.1.call-start
  123.6 1.5 slice.55
  125.1 0.0 reduce-scatter.6.cloned.1.call-start
  125.1 4.8 %slice.41 = f32[1024,1024]{0,1:T(8,128)} slice(f32[1024,1280]{0,1:T(8,128)} %copy-done.2), slice={[0:1024], [0:1024]} | slice | bytes 8388608 | tf_op jit(solution)/shard_map/slice | solution.py:112
  129.9 0.2 all-gather.7.cloned.1.call-start
  130.2 0.2 select_reduce_fusion
  130.4 0.1 select_reduce_fusion.1
  130.6 0.1 copy-done.1
  130.7 6.1 %gather_fusion.1 = s32[1024]{0:T(1024)S(1)} fusion(s32[8192]{0:T(1024)S(1)} %copy-done.1, s32[1024]{0:T(1024)S(1)} %broadcast_clamp_fusion.1), kind=kCustom, calls=%fused_computation.1 | custom fusion | bytes 12288 | tf_op jit(solution)/shard_map/jit(_take)/gather | solution.py:116
  136.8 0.1 compare_select_fusion
  136.9 45.5 %gather_fusion = s32[8192]{0:T(1024)S(1)} fusion(s32[8192]{0:T(1024)S(1)} %copy-done.1, s32[8192]{0:T(1024)S(1)} %broadcast_clamp_fusion), kind=kCustom, calls=%fused_computation | custom fusion | bytes 98304 | tf_op jit(solution)/shard_map/jit(_take)/gather | solution.py:60
  182.5 17.9 %all-gather.9.cloned.1.call-done = bf16[8192,1,128]{0,2,1:T(8,128)(2,1)} async-done(((bf16[128,1,128]{0,2,1:T(8,128)(2,1)}), bf16[8192,1,128]{0,2,1:T(8,128)(2,1)}) %all-gather.9.cloned.1.call-update) | async-done | bytes 2097168 | tf_op jit(solution)/shard_map/all_gather | solution.py:142
  200.4 4.1 copy.22
  204.5 69.9 %all-gather.5.cloned.1.call-done = bf16[8192,128]{0,1:T(8,128)(2,1)} async-done(((bf16[128,128]{0,1:T(8,128)(2,1)}), bf16[8192,128]{0,1:T(8,128)(2,1)}) %all-gather.5.cloned.1.call-update) | async-done | bytes 2097168 | tf_op jit(solution)/shard_map/all_gather | solution.py:143
  274.4 4.1 copy.23
  278.5 52.2 %reduce-scatter.6.cloned.1.call-done = f32[1024,128]{0,1:T(8,128)} async-done(((f32[1024,1024]{0,1:T(8,128)}), f32[1024,128]{0,1:T(8,128)}) %reduce-scatter.6.cloned.1.call-update) | async-done | bytes 524304 | tf_op jit(solution)/shard_map/reduce_scatter | solution.py:119
  330.7 2.1 fusion.36
  332.8 0.8 copy.19
  333.7 55.2 %while.15 = (s32[]{:T(128)}, f32[1,1024]{1,0:T(1,128)S(1)}, f32[1,1024]{1,0:T(1,128)S(1)}, f32[1,1024,128]{2,1,0:T(8,128)S(1)}, s32[8,1024]{1,0:T(8,128)S(1)}, /...) while((s32[]{:T(128)}, f32[1,1024]{1,0:T(1,128)S(1)}, ...), condition=%wide.region_9.10_spmd.clone, body=%wide.region_6.9_spmd.clone.sunk | while | flops 560337920 | bytes 14549149 | solution.py:92
  333.7 2.4 fusion.77
  336.1 1.6 fusion.79
  337.7 2.8 fusion.81
  340.6 2.4 fusion.77
  343.0 1.6 fusion.79
  344.6 2.8 fusion.81
  347.5 2.4 fusion.77
  349.9 1.6 fusion.79
  351.5 2.8 fusion.81
  354.4 2.4 fusion.77
  356.8 1.6 fusion.79
  358.4 2.8 fusion.81
  361.3 2.4 fusion.77
  363.7 1.6 fusion.79
  365.3 2.8 fusion.81
  368.2 2.4 fusion.77
  370.6 1.6 fusion.79
  372.2 2.8 fusion.81
  375.1 2.4 fusion.77
  377.5 1.6 fusion.79
  379.2 2.8 fusion.81
  382.0 2.4 fusion.77
  384.4 1.6 fusion.79
  386.1 2.8 fusion.81
  388.9 0.9 divide_convert_fusion
  389.8 0.0 reduce-scatter.8.cloned.1.call-start
  389.9 36.0 %all-gather.7.cloned.1.call-done = bf16[8,1024,128]{2,1,0:T(8,128)(2,1)} async-done(((bf16[1,1024,128]{2,1,0:T(8,128)(2,1)}), bf16[8,1024,128]{2,1,0:T(8,128)(2,1)}) %all-gather.7.cloned.1.call-update) | async-done | bytes 2097168 | tf_op jit(solution)/shard_map/all_gather | solution.py:152
  425.9 5.9 %bitcast_convert_fusion = bf16[1024,1024]{1,0:T(8,128)(2,1)} fusion(bf16[8,1024,128]{2,1,0:T(8,128)(2,1)} %all-gather.7.cloned.1.call-done, bf16[8,128,1024]{2,1,0:T(8,128)(2,1)} %bitcast.121), kind=kOutput, calls=%fused_computation.37 | convolution fusion | flops 2148532224 | bytes 6291456 | tf_op jit(solution)/shard_map/hqd,hdn->qn/dot_general | solution.py:150
  431.8 34.7 %reduce-scatter.8.cloned.1.call-done = bf16[256,1024]{1,0:T(8,128)(2,1)} async-done(((bf16[1024,1024]{1,0:T(8,128)(2,1)}), bf16[256,1024]{1,0:T(8,128)(2,1)}) %reduce-scatter.8.cloned.1.call-update) | async-done | bytes 524304 | tf_op jit(solution)/shard_map/reduce_scatter | solution.py:156
  (63 shorter events, 0.7 us)
Async XLA Ops:
  6.5 74.7 %copy-start = (bf16[1024,1,1280]{2,0,1:T(8,128)(2,1)S(1)}, bf16[1024,1,1280]{2,0,1:T(8,128)(2,1)}, u32[]{:S(2)}) copy-start(bf16[1024,1,1280]{2,0,1:T(8,128)(2,1)} %param.10) | copy-start | bytes 7864324
  6.5 115.3 %reduce-scatter.4.cloned.1.call-start = ((), (), s32[]{:S(2)}) async-start(), calls=%async_computation.4 | async-start | bytes 1179648 | tf_op jit(solution)/shard_map/reduce_scatter | solution.py:120
  81.3 8.2 %copy-start.3 = (s32[16]{0:T(128)S(1)}, s32[16]{0:T(128)}, u32[]{:S(2)}) copy-start(s32[16]{0:T(128)} %param.13) | copy-start | bytes 196
  86.0 2.3 copy-start.2
  89.3 111.1 %all-gather.9.cloned.1.call-start = ((), (), s32[]{:S(2)}) async-start(), calls=%async_computation.9 | async-start | bytes 2129920 | tf_op jit(solution)/shard_map/all_gather | solution.py:142
  123.5 150.9 %all-gather.5.cloned.1.call-start = ((), (), s32[]{:S(2)}) async-start(), calls=%async_computation.6 | async-start | bytes 2129920 | tf_op jit(solution)/shard_map/all_gather | solution.py:143
  125.1 205.6 %reduce-scatter.6.cloned.1.call-start = ((), (), s32[]{:S(2)}) async-start(), calls=%async_computation.5 | async-start | bytes 4718592 | tf_op jit(solution)/shard_map/reduce_scatter | solution.py:119
  129.9 0.8 copy-start.1
  129.9 296.0 %all-gather.7.cloned.1.call-start = ((), (), s32[]{:S(2)}) async-start(), calls=%async_computation.7 | async-start | bytes 2359296 | tf_op jit(solution)/shard_map/all_gather | solution.py:152
  389.8 76.7 %reduce-scatter.8.cloned.1.call-start = ((), (), s32[]{:S(2)}) async-start(), calls=%async_computation.8 | async-start | bytes 2621440 | tf_op jit(solution)/shard_map/reduce_scatter | solution.py:156
Sparse Core Ops, SparseCore 0:
  89.5 32.3 reduce-scatter.3
  124.4 75.9 all-gather.8
  203.0 71.3 all-gather.4
  276.8 53.8 reduce-scatter.5
  389.9 35.9 all-gather.6
  431.9 34.5 reduce-scatter.7
where the time goes:
time: 474 us; the launch traced here: 473 us
  waiting for transfers between devices  243 us (51%)
  local copies, waits for them, and re-layouts  79.3 us (17%)
  blocking collectives  58.6 us (12%)
  matrix products  51.9 us (11%)
  other arithmetic  25.8 us (5%)
  between operations  13.7 us (3%)
    all_gather x1, waiting for transfers between devices, on_device(): lax.all_gather(values_local, ('blk', 'uly'), axis=0, tiled=True)  69.9 us
    all_to_all x1, blocking collectives, on_device(): lax.all_to_all(rms_scaled, 'uly', split_axis=1, concat_axis=0, tiled=True)  58.6 us
    reduce_scatter x1, waiting for transfers between devices, on_device(): lax.psum_scatter(query_part, 'uly', scatter_dimension=1, tiled=True)  52.2 us
    gather x2, local copies, waits for them, and re-layouts, attend(): piece_seg = jnp.take(doc_ids, piece_pos)  45.5 us
    all_gather x1, waiting for transfers between devices, on_device(): lax.all_gather(attended, 'uly', axis=0, tiled=True)  36 us
    reduce_scatter x1, waiting for transfers between devices, on_device(): lax.psum_scatter(projected_rows.astype(jnp.bfloat16), 'tp', scatter_dimen...  34.7 us
    reduce_scatter x1, waiting for transfers between devices, on_device(): lax.psum_scatter(pair_part, 'uly', scatter_dimension=0, tiled=True)  32.3 us
    dot_general x8, matrix products, one_block(): jnp.einsum('hqk,kd->hqd', weights.astype(jnp.bfloat16), value_blk, prefer...  22.4 us
  transfers between devices with their start and end apart: 6, of which 6 were waited for; matrix products, arithmetic and copies ran while one was open for 14% of the time, Pallas kernels for 0%

commit v1 on v0

--- a/solution.py
+++ b/solution.py
@@ -10,6 +10,25 @@
 BLOCK = 512
 THETA = 500000.0
 NEG_BIG = -1e30
+
+
+def list_the_sheets(arr_in, on_dim, xs):
+    w1 = jax.lax.psum(1, "uly")
+    state_next, z, block_last = (w1, jax.lax.axis_index("uly"), arr_in.shape[on_dim])
+    buffer = tuple(((at, (at + 1) % state_next) for at in range(state_next)))
+    fields = tuple(((at, (at - 1) % state_next) for at in range(state_next)))
+    main = right_arr = arr_in
+    m_next = xs(arr_in, z * block_last)
+    e_now = state_next // 2
+    for k0 in range(1, e_now + 1):
+        main = jax.lax.ppermute(main, "uly", buffer)
+        if k0 < state_next - e_now:
+            right_arr = jax.lax.ppermute(right_arr, "uly", fields)
+            plain = xs(right_arr, (z + k0) % state_next * block_last)
+            m_next = m_next + plain
+        big = xs(main, (z - k0) % state_next * block_last)
+        m_next = m_next + big
+    return m_next
 
 
 def rope_tables(positions):
@@ -147,11 +166,15 @@
     row_max, row_sum, weighted = final_state
     attended = (weighted / row_sum[:, :, None]).astype(jnp.bfloat16)
     head_weights = w_out.reshape(group_width, HEAD_SIZE, w_out.shape[1])
-    projected_rows = jnp.einsum(
-        "hqd,hdn->qn",
-        lax.all_gather(attended, "uly", axis=0, tiled=True),
-        head_weights,
-        preferred_element_type=jnp.float32,
+    projected_rows = list_the_sheets(
+        attended,
+        0,
+        lambda own_block, at: jnp.einsum(
+            "hqd,hdn->qn",
+            own_block,
+            lax.dynamic_slice_in_dim(head_weights, at, own_block.shape[0], axis=0),
+            preferred_element_type=jnp.float32,
+        ),
     )
     return lax.psum_scatter(
         projected_rows.astype(jnp.bfloat16), "tp", scatter_dimension=0, tiled=True

time: 474 us -> 468 us (0.987)
  waiting for transfers between devices: 243 us -> 218 us
  matrix products: 51.9 us -> 64.3 us
  starting transfers between devices: 0.39 us -> 8.45 us
    all_gather x1 -> x0, waiting for transfers between devices: 36 us -> none  [on_device(): lax.all_gather(attended, 'uly', axis=0, tiled=True)]
    dot_general x1 -> x8, matrix products: 5.86 us -> 19.1 us  [on_device(): jnp.einsum('hqd,hdn->qn', own_block, lax.dynamic_slice_in_dim(head_weight...]
    ppermute x0 -> x7, waiting for transfers between devices: none -> 10 us  [the longest x4 10 us: list_the_sheets(): main = jax.lax.ppermute(main, 'uly', buffer)]
    ppermute x0 -> x7, starting transfers between devices: none -> 8.1 us  [the longest x3 8.01 us: list_the_sheets(): right_arr = jax.lax.ppermute(right_arr, 'uly', fields)]
    unnamed x12 -> x16, local copies, waits for them, and re-layouts: 15.4 us -> 14.7 us
  transfers between devices with their start and end apart: 6 -> 12, of which waited for: 6 -> 9; matrix products, arithmetic and copies ran while one was open for 14% -> 17% of each run, Pallas kernels for 0% -> 0%
where the time goes in v1:
time: 468 us; the launch traced here: 467 us
  waiting for transfers between devices  218 us (47%)
  local copies, waits for them, and re-layouts  78.6 us (17%)
  matrix products  64.3 us (14%)
  blocking collectives  58.6 us (13%)
  other arithmetic  25.1 us (5%)
  between operations  13.6 us (3%)
  starting transfers between devices  8.45 us (2%)
    all_gather x1, waiting for transfers between devices, on_device(): lax.all_gather(values_local, ('blk', 'uly'), axis=0, tiled=True)  69.9 us
    all_to_all x1, blocking collectives, on_device(): lax.all_to_all(rms_scaled, 'uly', split_axis=1, concat_axis=0, tiled=True)  58.6 us
    reduce_scatter x1, waiting for transfers between devices, on_device(): lax.psum_scatter(query_part, 'uly', scatter_dimension=1, tiled=True)  52.2 us
    gather x2, local copies, waits for them, and re-layouts, attend(): piece_seg = jnp.take(doc_ids, piece_pos)  45.5 us
    reduce_scatter x1, waiting for transfers between devices, on_device(): lax.psum_scatter(projected_rows.astype(jnp.bfloat16), 'tp', scatter_dimen...  35.2 us
    reduce_scatter x1, waiting for transfers between devices, on_device(): lax.psum_scatter(pair_part, 'uly', scatter_dimension=0, tiled=True)  32.3 us
    dot_general x8, matrix products, one_block(): jnp.einsum('hqk,kd->hqd', weights.astype(jnp.bfloat16), value_blk, prefer...  22.4 us
    dot_general x8, matrix products, on_device(): jnp.einsum('hqd,hdn->qn', own_block, lax.dynamic_slice_in_dim(head_weight...  19.1 us
  transfers between devices with their start and end apart: 12, of which 9 were waited for; matrix products, arithmetic and copies ran while one was open for 17% of the time, Pallas kernels for 0%

profile of v1, /device:TPU:1, one launch (start us, length us, event | category | flops | bytes accessed | tf_op | source)
XLA Modules:
  0.0 466.7 jit_solution(15015871772600722391)
XLA Ops:
  6.5 0.9 convert_element_type.57
  7.4 4.1 copy.12
  11.5 2.7 fusion.26
  14.2 4.6 fusion.28
  18.8 58.6 %all_to_all.19 = bf16[128,8,1024]{0,2,1:T(8,128)(2,1)} all-to-all(bf16[128,8,1024]{0,2,1:T(8,128)(2,1)S(1)} %bitcast.143), channel_id=1, replica_groups=mesh['blk'=8,'uly'=8,'tp'=4] {'uly'}, dimensions={1} | all-to-all | bytes 4194304 | tf_op jit(solution)/shard_map/all_to_all | solution.py:125
  77.4 3.9 copy.13
  81.3 4.7 %fusion.29 = f32[1024,1280]{0,1:T(8,128)S(1)} fusion(bf16[1024,1024]{1,0:T(8,128)(2,1)} %bitcast.155, bf16[1024,1,1280]{2,0,1:T(8,128)(2,1)S(1)} %copy-done), kind=kOutput, calls=%fused_computation.38 | convolution fusion | flops 2684354560 | bytes 9961472 | tf_op jit(solution)/shard_map/dot_general | solution.py:130
  86.0 2.3 copy-done.3
  88.2 1.1 slice.37
  89.6 32.3 %reduce-scatter.4.cloned.1.call-done = f32[128,256]{0,1:T(8,128)} async-done(((f32[1024,256]{0,1:T(8,128)}), f32[128,256]{0,1:T(8,128)}) %reduce-scatter.4.cloned.1.call-update) | async-done | bytes 131088 | tf_op jit(solution)/shard_map/reduce_scatter | solution.py:139
  121.8 0.8 slice_bitcast_fusion
  122.9 0.6 pad_maximum_fusion.1
  123.6 1.5 slice.55
  125.1 4.8 %slice.41 = f32[1024,1024]{0,1:T(8,128)} slice(f32[1024,1280]{0,1:T(8,128)} %copy-done.3), slice={[0:1024], [0:1024]} | slice | bytes 8388608 | tf_op jit(solution)/shard_map/slice | solution.py:131
  129.9 0.2 reduce-scatter.8.cloned.1.call-start
  130.7 6.2 %gather_fusion.1 = s32[1024]{0:T(1024)S(1)} fusion(s32[8192]{0:T(1024)S(1)} %copy-done.2, s32[1024]{0:T(1024)S(1)} %broadcast_clamp_fusion.1), kind=kCustom, calls=%fused_computation.1 | custom fusion | bytes 12288 | tf_op jit(solution)/shard_map/jit(_take)/gather | solution.py:135
  137.0 45.5 %gather_fusion = s32[8192]{0:T(1024)S(1)} fusion(s32[8192]{0:T(1024)S(1)} %copy-done.2, s32[8192]{0:T(1024)S(1)} %broadcast_clamp_fusion), kind=kCustom, calls=%fused_computation | custom fusion | bytes 98304 | tf_op jit(solution)/shard_map/jit(_take)/gather | solution.py:79
  182.6 17.9 %all-gather.6.cloned.1.call-done = bf16[8192,1,128]{0,2,1:T(8,128)(2,1)} async-done(((bf16[128,1,128]{0,2,1:T(8,128)(2,1)}), bf16[8192,1,128]{0,2,1:T(8,128)(2,1)}) %all-gather.6.cloned.1.call-update) | async-done | bytes 2097168 | tf_op jit(solution)/shard_map/all_gather | solution.py:161
  200.5 4.1 copy.20
  204.6 69.9 %all-gather.4.cloned.1.call-done = bf16[8192,128]{0,1:T(8,128)(2,1)} async-done(((bf16[128,128]{0,1:T(8,128)(2,1)}), bf16[8192,128]{0,1:T(8,128)(2,1)}) %all-gather.4.cloned.1.call-update) | async-done | bytes 2097168 | tf_op jit(solution)/shard_map/all_gather | solution.py:162
  274.5 4.1 copy.21
  278.5 52.2 %reduce-scatter.6.cloned.1.call-done = f32[1024,128]{0,1:T(8,128)} async-done(((f32[1024,1024]{0,1:T(8,128)}), f32[1024,128]{0,1:T(8,128)}) %reduce-scatter.6.cloned.1.call-update) | async-done | bytes 524304 | tf_op jit(solution)/shard_map/reduce_scatter | solution.py:138
  330.7 2.1 fusion.36
  333.1 54.4 %while.15 = (s32[]{:T(128)}, f32[1,1024]{1,0:T(1,128)S(1)}, f32[1,1024]{1,0:T(1,128)S(1)}, f32[1,1024,128]{2,1,0:T(8,128)S(1)}, s32[8,1024]{1,0:T(8,128)S(1)}, /...) while((s32[]{:T(128)}, f32[1,1024]{1,0:T(1,128)S(1)}, ...), condition=%wide.region_9.10_spmd.clone, body=%wide.region_6.9_spmd.clone.sunk | while | flops 560337920 | bytes 14549149 | solution.py:111
  333.1 2.4 fusion.114
  335.5 1.6 fusion.116
  337.2 2.8 fusion.118
  340.0 2.3 fusion.114
  342.3 1.6 fusion.116
  344.0 2.8 fusion.118
  346.8 2.2 fusion.114
  349.1 1.6 fusion.116
  350.8 2.8 fusion.118
  353.6 2.3 fusion.114
  355.9 1.6 fusion.116
  357.5 2.8 fusion.118
  360.4 2.2 fusion.114
  362.7 1.6 fusion.116
  364.3 2.8 fusion.118
  367.2 2.3 fusion.114
  369.5 1.6 fusion.116
  371.1 2.8 fusion.118
  374.0 2.2 fusion.114
  376.2 1.6 fusion.116
  377.9 2.8 fusion.118
  380.7 2.3 fusion.114
  383.0 1.6 fusion.116
  384.7 2.8 fusion.118
  387.8 2.7 collective-permute-start
  390.5 0.7 fusion.59
  391.2 5.1 %collective-permute-done.1 = bf16[1,1024,128]{2,1,0:T(8,128)(2,1)S(1)} collective-permute-done((bf16[1,1024,128]{2,1,0:T(8,128)(2,1)S(1)}, bf16[1,1024,128]{2,1,0:T(8,128)(2,1)S(1)}, u32[]{:S(2)}, u32[]{:S(2)}) %collective-permute-start.1) | collective-permute-done | bytes 262176 | tf_op jit(solution)/shard_map/ppermute | solution.py:24
  396.2 2.7 collective-permute-start.2
  398.9 0.7 fusion.56
  399.6 0.7 fusion.53
  400.3 3.4 collective-permute-done.3
  403.8 2.7 collective-permute-start.4
  406.4 0.7 fusion.50
  407.1 2.7 fusion.47
  409.8 0.4 collective-permute-done.5
  410.2 2.6 fusion.41
  412.8 2.7 fusion.44
  415.5 1.1 collective-permute-done.6
  416.6 8.3 %add_convert_fusion = bf16[1024,1024]{1,0:T(8,128)(2,1)} fusion(f32[1024,1024]{1,0:T(8,128)} %fusion.41, f32[1024,1024]{1,0:T(8,128)} %fusion.44, f32[1024,1024]{1,0:T(8,128)} %fusion.47, f32[1024,1024]{1,0:T(8,128)S(1)} %fusion.50, f32[1024,1024]{1,0:T(8,128)S(1)} %fusion.53, f32[1024,1024]{1,0:T(8,128)S(1)} %fusion.59, f32[1024,1024]{1,0:T(8,128)S(1)} %fusion.56, ...), kind=kOutput, calls=%fused_computation.37 | convolution fusion | flops 276824064 | bytes 31981572 | tf_op jit(solution)/shard_map/hqd,hdn->qn/dot_general | solution.py:172
  425.0 35.2 %reduce-scatter.8.cloned.1.call-done = bf16[256,1024]{1,0:T(8,128)(2,1)} async-done(((bf16[1024,1024]{1,0:T(8,128)(2,1)}), bf16[256,1024]{1,0:T(8,128)(2,1)}) %reduce-scatter.8.cloned.1.call-update) | async-done | bytes 524304 | tf_op jit(solution)/shard_map/reduce_scatter | solution.py:179
  (85 shorter events, 1.9 us)
Async XLA Ops:
  6.5 74.7 %copy-start = (bf16[1024,1,1280]{2,0,1:T(8,128)(2,1)S(1)}, bf16[1024,1,1280]{2,0,1:T(8,128)(2,1)}, u32[]{:S(2)}) copy-start(bf16[1024,1,1280]{2,0,1:T(8,128)(2,1)} %param.10) | copy-start | bytes 7864324
  6.5 115.3 %reduce-scatter.4.cloned.1.call-start = ((), (), s32[]{:S(2)}) async-start(), calls=%async_computation.4 | async-start | bytes 1179648 | tf_op jit(solution)/shard_map/reduce_scatter | solution.py:139
  81.3 8.2 %copy-start.5 = (s32[16]{0:T(128)S(1)}, s32[16]{0:T(128)}, u32[]{:S(2)}) copy-start(s32[16]{0:T(128)} %param.13) | copy-start | bytes 196
  86.0 2.3 copy-start.3
  89.3 111.2 %all-gather.6.cloned.1.call-start = ((), (), s32[]{:S(2)}) async-start(), calls=%async_computation.8 | async-start | bytes 2129920 | tf_op jit(solution)/shard_map/all_gather | solution.py:161
  123.5 150.9 %all-gather.4.cloned.1.call-start = ((), (), s32[]{:S(2)}) async-start(), calls=%async_computation.6 | async-start | bytes 2129920 | tf_op jit(solution)/shard_map/all_gather | solution.py:162
  125.1 205.7 %reduce-scatter.6.cloned.1.call-start = ((), (), s32[]{:S(2)}) async-start(), calls=%async_computation.5 | async-start | bytes 4718592 | tf_op jit(solution)/shard_map/reduce_scatter | solution.py:138
  129.9 0.8 copy-start.2
  129.9 330.2 %reduce-scatter.8.cloned.1.call-start = ((), (), s32[]{:S(2)}) async-start(), calls=%async_computation.7 | async-start | bytes 2621440 | tf_op jit(solution)/shard_map/reduce_scatter | solution.py:179
  333.1 57.4 %copy-start.4 = (bf16[1024,1024]{1,0:T(8,128)(2,1)S(1)}, bf16[1024,1024]{1,0:T(8,128)(2,1)}, u32[]{:S(2)}) copy-start(bf16[1024,1024]{1,0:T(8,128)(2,1)} %param.11) | copy-start | bytes 6291460
  387.7 8.5 %collective-permute-start.1 = (bf16[1,1024,128]{2,1,0:T(8,128)(2,1)S(1)}, bf16[1,1024,128]{2,1,0:T(8,128)(2,1)S(1)}, u32[]{:S(2)}, u32[]{:S(2)}) collective-permute-start(bf16[1,1024,128]{2,1,0:T(8,128)(2,1)S(1)} %divide_convert_fusion), channel_id=1, source_target_pairs={{0,4},{4,8},{8,12},{12,16},{16,20},{20,24},{24,28},{28,0},{1,5},{5... | collective-permute-start | bytes 786440 | tf_op jit(solution)/shard_map/ppermute | solution.py:24
  387.8 8.4 %collective-permute-start = (bf16[1,1024,128]{2,1,0:T(8,128)(2,1)S(1)}, bf16[1,1024,128]{2,1,0:T(8,128)(2,1)S(1)}, u32[]{:S(2)}, u32[]{:S(2)}) collective-permute-start(bf16[1,1024,128]{2,1,0:T(8,128)(2,1)S(1)} %divide_convert_fusion), channel_id=1, source_target_pairs={{0,28},{4,0},{8,4},{12,8},{16,12},{20,16},{24,20},{28,24},{1,29},{... | collective-permute-start | bytes 786440 | tf_op jit(solution)/shard_map/ppermute | solution.py:26
  396.2 7.5 %collective-permute-start.3 = (bf16[1,1024,128]{2,1,0:T(8,128)(2,1)S(1)}, bf16[1,1024,128]{2,1,0:T(8,128)(2,1)S(1)}, u32[]{:S(2)}, u32[]{:S(2)}) collective-permute-start(bf16[1,1024,128]{2,1,0:T(8,128)(2,1)S(1)} %collective-permute-done.1), channel_id=1, source_target_pairs={{0,4},{4,8},{8,12},{12,16},{16,20},{20,24},{24,28},{28,0},{1,5},{5... | collective-permute-start | bytes 786440 | tf_op jit(solution)/shard_map/ppermute | solution.py:24
  396.2 7.5 %collective-permute-start.2 = (bf16[1,1024,128]{2,1,0:T(8,128)(2,1)S(1)}, bf16[1,1024,128]{2,1,0:T(8,128)(2,1)S(1)}, u32[]{:S(2)}, u32[]{:S(2)}) collective-permute-start(bf16[1,1024,128]{2,1,0:T(8,128)(2,1)S(1)} %collective-permute-done), channel_id=1, source_target_pairs={{0,28},{4,0},{8,4},{12,8},{16,12},{20,16},{24,20},{28,24},{1,29},{... | collective-permute-start | bytes 786440 | tf_op jit(solution)/shard_map/ppermute | solution.py:26
  403.8 6.4 %collective-permute-start.5 = (bf16[1,1024,128]{2,1,0:T(8,128)(2,1)S(1)}, bf16[1,1024,128]{2,1,0:T(8,128)(2,1)S(1)}, u32[]{:S(2)}, u32[]{:S(2)}) collective-permute-start(bf16[1,1024,128]{2,1,0:T(8,128)(2,1)S(1)} %collective-permute-done.3), channel_id=1, source_target_pairs={{0,4},{4,8},{8,12},{12,16},{16,20},{20,24},{24,28},{28,0},{1,5},{5... | collective-permute-start | bytes 786440 | tf_op jit(solution)/shard_map/ppermute | solution.py:24
  403.8 9.1 %collective-permute-start.4 = (bf16[1,1024,128]{2,1,0:T(8,128)(2,1)S(1)}, bf16[1,1024,128]{2,1,0:T(8,128)(2,1)S(1)}, u32[]{:S(2)}, u32[]{:S(2)}) collective-permute-start(bf16[1,1024,128]{2,1,0:T(8,128)(2,1)S(1)} %collective-permute-done.2), channel_id=1, source_target_pairs={{0,28},{4,0},{8,4},{12,8},{16,12},{20,16},{24,20},{28,24},{1,29},{... | collective-permute-start | bytes 786440 | tf_op jit(solution)/shard_map/ppermute | solution.py:26
  410.2 6.4 %collective-permute-start.6 = (bf16[1,1024,128]{2,1,0:T(8,128)(2,1)S(1)}, bf16[1,1024,128]{2,1,0:T(8,128)(2,1)S(1)}, u32[]{:S(2)}, u32[]{:S(2)}) collective-permute-start(bf16[1,1024,128]{2,1,0:T(8,128)(2,1)S(1)} %collective-permute-done.5), channel_id=1, source_target_pairs={{0,4},{4,8},{8,12},{12,16},{16,20},{20,24},{24,28},{28,0},{1,5},{5... | collective-permute-start | bytes 786440 | tf_op jit(solution)/shard_map/ppermute | solution.py:24
  416.6 43.5 %copy-start.1 = (bf16[1024,1,1280]{2,0,1:T(8,128)(2,1)S(1)}, bf16[1024,1,1280]{2,0,1:T(8,128)(2,1)}, u32[]{:S(2)}) copy-start(bf16[1024,1,1280]{2,0,1:T(8,128)(2,1)} %param.10) | copy-start | bytes 7864324
Sparse Core Ops, SparseCore 0:
  89.5 32.3 reduce-scatter.3
  124.4 76.0 all-gather.5
  203.1 71.3 all-gather.3
  276.9 53.8 reduce-scatter.5
  425.1 34.9 reduce-scatter.7
